TPU v7x, 32 devices: a whole 2x2x4 slice. The times are simulated.
32 devices in a mesh: freq: 2 (over x), trial: 16 (over z, y, core).
Axes of the slice: x: 2, y: 2, z: 4, core: 2. Of those that a mesh axis runs over, the one named last changes fastest.
Arguments:
- signals: bfloat16 [32, 306, 1024], P('trial'), may hold values from -6 to 6
- kernel: bfloat16 [8192, 306], P('trial'), may hold values from -0.3125 to 0.3125
- freqs: float32 [10], P('freq'), may hold values from 3.6 to 66
Outputs:
- rel_power: float32 [8192, 160], P('trial', 'freq')
- itc_score: float32 [8192, 160], P('trial', 'freq')
All inputs are finite; a program needn't handle non-finite values.
Results may differ from a plain program's by a relative error of at most 0.0003.
Values may be sent and summed in bfloat16 or wider, within the bound.
A program may use at most 64 MiB of HBM per device.

v0:
```python
import jax
import jax.numpy as jnp
from jax import lax
from jax.sharding import PartitionSpec as P

TOUT = 16


CYCLES = 7.0
SAMPLE_RATE = 1000.0
PHASE_FLOOR = 0.25
MEAN_EPSILON = 1e-06


def wavelet_table(frequencies, sample_count, point_count):
    stride = sample_count // point_count
    moments = jnp.arange(sample_count, dtype=frequencies.dtype)[:, None, None]
    centres = (jnp.arange(point_count, dtype=frequencies.dtype) * stride + stride // 2)[
        None, None, :
    ]
    widths = CYCLES * SAMPLE_RATE / (2.0 * jnp.pi) / frequencies[None, :, None]
    offset = moments - centres
    envelope = jnp.exp(-offset * offset / (2.0 * widths * widths)) * (8.0 / widths)
    angles = 2.0 * jnp.pi / SAMPLE_RATE * frequencies[None, :, None] * offset
    stacked = jnp.stack([envelope * jnp.cos(angles), envelope * jnp.sin(angles)], axis=1)
    return stacked.reshape(sample_count, -1)


def source_terms(kernel_rows, coefficients, span):
    source = jnp.einsum(
        "sc,ncm->snm",
        kernel_rows.astype(jnp.float32),
        coefficients,
        precision=lax.Precision.HIGHEST,
        preferred_element_type=jnp.float32,
    )
    real_part = source[:, :, :span]
    imag_part = source[:, :, span:]
    magnitude = real_part * real_part + imag_part * imag_part
    inverse = lax.rsqrt(magnitude + PHASE_FLOOR)
    return jnp.concatenate(
        [
            jnp.sum(magnitude, axis=1),
            jnp.sum(real_part * inverse, axis=1),
            jnp.sum(imag_part * inverse, axis=1),
        ],
        axis=1,
    )


def shards(signals, kernel, freqs):
    trial_count, chan_count, sample_count = signals.shape
    span = freqs.shape[0] * TOUT
    table = wavelet_table(freqs, sample_count, TOUT)
    flat = signals.reshape(trial_count * chan_count, sample_count)
    coefficients = jnp.dot(
        flat, table, precision=lax.Precision.HIGHEST, preferred_element_type=jnp.float32
    )
    coefficients = coefficients.reshape(trial_count, chan_count, 2 * span)
    all_trials = trial_count * lax.axis_size("trial")
    totals = source_terms(kernel, lax.all_gather(coefficients, "trial", axis=0, tiled=True), span)
    power = totals[:, :span] / all_trials
    phase_real = totals[:, span : 2 * span]
    phase_imag = totals[:, 2 * span :]
    source_sum = lax.psum(jnp.sum(power, axis=1), "freq")
    mean_power = source_sum / (span * lax.axis_size("freq"))
    rel_power = power / (mean_power[:, None] + MEAN_EPSILON)
    itc_score = (phase_real * phase_real + phase_imag * phase_imag) / all_trials
    return (rel_power, itc_score)


def solution(mesh):
    placed = (P("trial", None, None), P("trial", None), P("freq"))
    return jax.shard_map(
        shards,
        mesh=mesh,
        in_specs=placed,
        out_specs=(P("trial", "freq"), P("trial", "freq")),
        check_vma=False,
    )
```

profile of v0, /device:TPU:0, one launch (start us, length us, event | category | flops | bytes accessed | tf_op | source)
XLA Modules:
  0.0 113.3 jit_solution(2727243173726638218)
XLA Ops:
  7.2 0.0 copy-start
  7.2 0.0 all-gather.2.cloned.1.call-start
  7.2 0.7 multiply_multiply_fusion
  7.9 0.1 negate_multiply_fusion
  8.0 1.6 %copy.8 = bf16[2,306,1024]{2,1,0:T(8,128)(2,1)S(1)} copy(bf16[2,306,1024]{2,0,1:T(2,128)(2,1)} %param.3) | data formatting | bytes 2506752 | tf_op args[0]
  9.7 0.2 reshape.96
  9.9 1.3 %fusion.1 = (f32[1024,1,5,16]{0,3,2,1:T(8,128)S(1)}, f32[1024,1,5,16]{0,3,2,1:T(8,128)S(1)}) fusion(f32[1024,16]{0,1:T(8,128)S(1)} %get-tuple-element.8, f32[5]{0:T(128)S(1)} %get-tuple-element.10, f32[5]{0:T(128)S(1)} %get-tuple-element.11, f32[5]{0:T(128)S(1)} %get-tuple-element.9, f32[1024,16]{0,1:T(8,128)S(1)} %get-tuple-element.7), kind=kLoop, calls=%fused_computation.11 | loop fusion | flops 409600 | bytes 786492 | tf_op jit(solution)/shard_map/mul | solution.py:25
  11.2 0.1 pad_maximum_fusion
  11.3 1.3 %convolution_bitcast_fusion.1 = f32[612,160]{0,1:T(8,128)S(1)} fusion(f32[1024,160]{0,1:T(8,128)S(1)} %bitcast.13, bf16[612,1024]{1,0:T(8,128)(2,1)S(1)} %reshape.96), kind=kOutput, calls=%fused_computation.5 | convolution fusion | flops 1203240960 | bytes 2300416 | tf_op jit(solution)/shard_map/dot_general | solution.py:56
  12.6 0.4 reshape.97
  13.0 0.8 copy.9
  13.8 0.0 all-gather.2.cloned.1.call-update
  13.8 73.9 %all-gather.2.cloned.1.call-done = f32[32,306,160]{1,2,0:T(8,128)} async-done(((f32[2,306,160]{1,2,0:T(8,128)}), f32[32,306,160]{1,2,0:T(8,128)}) %all-gather.2.cloned.1.call-update) | async-done | bytes 6266896 | tf_op jit(solution)/shard_map/all_gather | solution.py:61
  87.7 0.0 copy-done
  87.7 10.6 %convolution_bitcast_fusion = f32[512,32,160]{0,2,1:T(8,128)S(1)} fusion(f32[32,306,160]{1,2,0:T(8,128)} %all-gather.2.cloned.1.call-done, bf16[512,306]{0,1:T(8,128)(2,1)S(1)} %copy-done), kind=kOutput, calls=%fused_computation.4 | convolution fusion | flops 9625927680 | bytes 17065984 | tf_op jit(solution)/shard_map/sc,ncm->snm/dot_general | solution.py:30
  98.3 1.8 %multiply_reduce_fusion.1 = (f32[512,80]{0,1:T(8,128)S(1)}, f32[512,80]{0,1:T(8,128)S(1)}, f32[512,80]{0,1:T(8,128)S(1)}) fusion(f32[512,32,160]{0,2,1:T(8,128)S(1)} %convolution_bitcast_fusion), kind=kLoop, calls=%fused_computation.1 | loop fusion | flops 11673600 | bytes 10977280 | tf_op jit(solution)/shard_map/reduce_sum | solution.py:44
  100.1 4.9 %psum.7 = f32[512]{0:T(512)S(1)} all-reduce(f32[512]{0:T(512)S(1)} %multiply_reduce_fusion.2), channel_id=1, replica_groups=mesh['freq'=2,'trial'=16] {'freq'}, use_global_device_ids=true, to_apply=%region_2.0 | all-reduce | flops 512 | bytes 4096 | tf_op jit(solution)/shard_map/psum | solution.py:65
  105.1 0.7 multiply_divide_fusion
  105.8 0.7 add_multiply_fusion
  (3 shorter events, 0.0 us)
Async XLA Ops:
  7.2 80.5 %copy-start = (bf16[512,306]{0,1:T(8,128)(2,1)S(1)}, bf16[512,306]{0,1:T(8,128)(2,1)}, u32[]{:S(2)}) copy-start(bf16[512,306]{0,1:T(8,128)(2,1)} %param.4) | copy-start | bytes 940036
  7.2 80.5 %all-gather.2.cloned.1.call-start = ((), (), s32[]{:S(2)}) async-start(), calls=%async_computation | async-start | bytes 8355840 | tf_op jit(solution)/shard_map/all_gather | solution.py:61
Sparse Core Ops, SparseCore 0:
  13.9 73.6 all-gather.1
where the time goes:
time: 113 us
  waiting for transfers between devices  73.9 us (65%)
  between operations  14.1 us (12%)
  matrix products  12 us (11%)
  other arithmetic  5.31 us (5%)
  blocking collectives  4.93 us (4%)
  local copies, waits for them, and re-layouts  3.08 us (3%)
    all_gather x1, waiting for transfers between devices, shards(): lax.all_gather(coefficients, 'trial', axis=0, tiled=True)  73.9 us
    dot_general x1, matrix products, source_terms(): jnp.einsum('sc,ncm->snm', kernel_rows.astype(jnp.float32), coefficients,...  10.6 us
    psum x1, blocking collectives, shards(): source_sum = lax.psum(jnp.sum(power, axis=1), 'freq')  4.93 us
  transfers between devices with their start and end apart: 1, of which 1 were waited for; matrix products, arithmetic and copies ran while one was open for 0% of the time, Pallas kernels for 0%

commit v1 on v0

v1 whole, which is shorter than its diff:
```python
import functools
import math

import jax
import jax.numpy as jnp
from jax import lax
from jax.experimental import pallas as pl
from jax.experimental.pallas import tpu as pltpu
from jax.sharding import PartitionSpec as P

TOUT = 16
CYCLES = 7.0
SAMPLE_RATE = 1000.0
PHASE_FLOOR = 0.25
MEAN_EPSILON = 1e-06
LANES = 128
MESH = pl.DeviceIdType.MESH
F32 = jnp.float32
BF16 = jnp.bfloat16


def grid_of(chips):
    outer = 1
    while outer * outer < chips or chips % outer:
        outer += 1
    return outer, chips // outer


def polynomial(x2, terms):
    total = jnp.full_like(x2, terms[-1])
    for term in reversed(terms[:-1]):
        total = total * x2 + term
    return total


SIN_TERMS = [(-1) ** i * math.pi ** (2 * i + 1) / math.factorial(2 * i + 1) for i in range(8)]
COS_TERMS = [(-1) ** i * math.pi ** (2 * i) / math.factorial(2 * i) for i in range(8)]


def wavelet_rows(freq, points, samples):
    stride = samples // points
    moments = lax.broadcasted_iota(jnp.int32, (points, samples), 1)
    centres = lax.broadcasted_iota(jnp.int32, (points, samples), 0) * stride + stride // 2
    scaled = (moments - centres).astype(F32) * freq
    rate = 2.0 * math.pi / (CYCLES * SAMPLE_RATE)
    envelope = jnp.exp(scaled * scaled * (-0.5 * rate * rate)) * (freq * (8.0 * rate))
    turns = scaled * (1.0 / SAMPLE_RATE)
    part = turns - jnp.floor(turns + 0.5)
    square = part * part
    half_sin = part * polynomial(square, SIN_TERMS)
    half_cos = polynomial(square, COS_TERMS)
    return (
        envelope * (1.0 - 2.0 * half_sin * half_sin),
        envelope * (2.0 * half_sin * half_cos),
    )


def split(x):
    high = x.astype(BF16)
    return high, (x - high.astype(F32)).astype(BF16)


def encode(rows):
    return split(rows)


def decode(block):
    return block[0], block[1]


def body(
    outer,
    inner,
    groups,
    freqs_ref,
    signals_ref,
    kernel_ref,
    rel_ref,
    itc_ref,
    table,
    rest_rows,
    blocks,
    peer_kernel,
    rest_pad,
    weights,
    acc,
    peer_acc,
    sums,
    out_sums,
    recv,
    outer_send,
    inner_send,
    pair_send,
    pair_recv,
    sum_send,
    sum_recv,
):
    local, chans, samples = signals_ref.shape
    sources = kernel_ref.shape[0]
    bands = freqs_ref.shape[0]
    span = bands * TOUT
    main = chans // LANES * LANES
    rest = chans - main
    slot_rows = LANES // local
    chunks = blocks.shape[1]

    group = lax.axis_index("freq")
    place = lax.axis_index("trial")
    core = place % 2
    chip = place // 2
    a = chip // inner
    b = chip % inner
    partner = place + 1 - 2 * core

    def at(oa, ob):
        return (oa * inner + ob) * 2 + core

    barrier = pltpu.get_barrier_semaphore()

    def greet(target):
        pl.semaphore_signal(barrier, inc=1, device_id=target, device_id_type=MESH)

    for ahead in (-1, 1):
        ia = a + ahead
        ib = b + ahead

        @pl.when((ia >= 0) & (ia < outer))
        def _():
            greet({"trial": at(ia, b)})

        @pl.when((ib >= 0) & (ib < inner))
        def _():
            greet({"trial": at(a, ib)})

    others = []
    for step in range(groups):
        for flip in range(2):
            if step or flip:
                others.append((step, flip))

    def other(step, flip):
        there = (group + step) % groups
        seat = partner if flip else place
        return {"freq": there, "trial": seat}

    for step, flip in others:
        greet(other(step, flip))
    near = (
        jnp.minimum(a, 1)
        + jnp.minimum(outer - 1 - a, 1)
        + jnp.minimum(b, 1)
        + jnp.minimum(inner - 1 - b, 1)
    )
    pl.semaphore_wait(barrier, near + len(others))

    kernel_copy = pltpu.make_async_remote_copy(
        src_ref=kernel_ref,
        dst_ref=peer_kernel,
        send_sem=pair_send.at[0],
        recv_sem=pair_recv.at[0],
        device_id={"trial": partner},
        device_id_type=MESH,
    )
    kernel_copy.start()

    for band in range(bands):
        cos_rows, sin_rows = wavelet_rows(freqs_ref[band], TOUT, samples)
        for half, rows in enumerate((cos_rows, sin_rows)):
            high, low = split(rows)
            first = half * span + band * TOUT
            table[first : first + TOUT, :] = high
            table[2 * span + first : 2 * span + first + TOUT, :] = low
    rest_rows[...] = jnp.zeros_like(rest_rows)
    for j in range(local):
        rest_rows[j * slot_rows : j * slot_rows + rest, :] = signals_ref[j, main:chans, :]

    mine = a * inner + b
    pieces = [(j * main, main, functools.partial(lambda j: signals_ref[j, 0:main, :], j)) for j in range(local)]
    pieces.append((local * main, LANES, lambda: rest_rows[...]))
    for start, width, load in pieces:
        both = lax.dot_general(
            table[...], load(), (((1,), (1,)), ((), ())), preferred_element_type=F32
        )
        coded = encode(both[: 2 * span] + both[2 * span :])
        for chunk in range(chunks):
            blocks[mine, chunk, :, start : start + width] = coded[chunk]

    def outer_copy(oa, chunk, ahead):
        slot = oa * inner + b
        side = (ahead + 1) // 2
        return pltpu.make_async_remote_copy(
            src_ref=blocks.at[slot, chunk],
            dst_ref=blocks.at[slot, chunk],
            send_sem=outer_send.at[side, oa, chunk],
            recv_sem=recv.at[slot, chunk],
            device_id={"trial": at(a + ahead, b)},
            device_id_type=MESH,
        )

    def inner_copy(oa, ob, chunk, ahead):
        slot = oa * inner + ob
        side = (ahead + 1) // 2
        return pltpu.make_async_remote_copy(
            src_ref=blocks.at[slot, chunk],
            dst_ref=blocks.at[slot, chunk],
            send_sem=inner_send.at[side, slot, chunk],
            recv_sem=recv.at[slot, chunk],
            device_id={"trial": at(a, b + ahead)},
            device_id_type=MESH,
        )

    def outer_sends(oa, chunk, act):
        @pl.when((oa <= a) & (a + 1 < outer))
        def _():
            act(outer_copy(oa, chunk, 1))

        @pl.when((oa >= a) & (a >= 1))
        def _():
            act(outer_copy(oa, chunk, -1))

    def inner_sends(oa, ob, chunk, act):
        @pl.when((ob <= b) & (b + 1 < inner))
        def _():
            act(inner_copy(oa, ob, chunk, 1))

        @pl.when((ob >= b) & (b >= 1))
        def _():
            act(inner_copy(oa, ob, chunk, -1))

    def start(copy):
        copy.start()

    def finish(copy):
        copy.wait_send()

    def nearest(k, here, count):
        left = here
        right = count - 1 - here
        both = 2 * jnp.minimum(left, right)
        dist = jnp.where(k <= both, (k + 1) // 2, k - both // 2)
        to_left = jnp.where(k <= both, k % 2, jnp.where(left > right, 1, 0))
        return here + dist - 2 * dist * to_left

    for chunk in range(chunks):
        outer_sends(a, chunk, start)
        inner_sends(a, b, chunk, start)

    acc[...] = jnp.zeros_like(acc)

    def place_weights(ref, first):
        wide = ref[:, 0:main].astype(F32).T.astype(BF16)
        rest_pad[...] = jnp.zeros_like(rest_pad)
        rest_pad[:, 0:rest] = ref[:, main:chans].astype(F32)
        tail = rest_pad[...].T.astype(BF16)[0:slot_rows]
        cols = slice(first, first + sources)
        for j in range(local):
            for copy in range(2):
                weights[j, copy * main : (copy + 1) * main, cols] = wide
                base = 2 * main + copy * LANES
                for other_slot in range(local):
                    rows = slice(base + other_slot * slot_rows, base + (other_slot + 1) * slot_rows)
                    weights[j, rows, cols] = tail if other_slot == j else jnp.zeros_like(tail)

    place_weights(kernel_ref, 0)
    kernel_copy.wait()
    place_weights(peer_kernel, sources)

    step_lanes = min(256, sources)
    tiles = sources // step_lanes

    def compute(slot):
        high, low = decode([blocks[slot, chunk] for chunk in range(chunks)])
        tail = local * main
        for j in range(local):
            left = jnp.concatenate(
                [
                    high[:, j * main : (j + 1) * main],
                    low[:, j * main : (j + 1) * main],
                    high[:, tail : tail + LANES],
                    low[:, tail : tail + LANES],
                ],
                axis=1,
            )
            for half in range(2):
                for tile in range(tiles):
                    lanes = slice(tile * step_lanes, (tile + 1) * step_lanes)
                    first = half * sources + tile * step_lanes
                    source = jnp.dot(
                        left,
                        weights[j, :, first : first + step_lanes],
                        preferred_element_type=F32,
                    )
                    real = source[:span]
                    imag = source[span:]
                    magnitude = real * real + imag * imag
                    inverse = lax.rsqrt(magnitude + PHASE_FLOOR)
                    acc[half, 0, :, lanes] += magnitude
                    acc[half, 1, :, lanes] += real * inverse
                    acc[half, 2, :, lanes] += imag * inverse

    def arrived(slot, chunk):
        pltpu.make_async_remote_copy(
            src_ref=blocks.at[slot, chunk],
            dst_ref=blocks.at[slot, chunk],
            send_sem=pair_send.at[0],
            recv_sem=recv.at[slot, chunk],
            device_id={"trial": partner},
            device_id_type=MESH,
        ).wait_recv()

    def event(e, carry):
        ka = e // inner
        kb = e % inner
        oa = nearest(ka, a, outer)
        ob = nearest(kb, b, inner)

        @pl.when(kb > 0)
        def _():
            for chunk in range(chunks):
                arrived(oa * inner + ob, chunk)
                inner_sends(oa, ob, chunk, start)

        compute(oa * inner + ob)

        @pl.when((kb == 0) & (ka + 1 < outer))
        def _():
            na = nearest(ka + 1, a, outer)
            for chunk in range(chunks):
                arrived(na * inner + b, chunk)
                outer_sends(na, chunk, start)
                inner_sends(na, b, chunk, start)

        return carry

    lax.fori_loop(0, outer * inner, event, 0)

    pair_copy = pltpu.make_async_remote_copy(
        src_ref=acc.at[1],
        dst_ref=peer_acc,
        send_sem=pair_send.at[1],
        recv_sem=pair_recv.at[1],
        device_id={"trial": partner},
        device_id_type=MESH,
    )
    pair_copy.start()
    for half in range(2):
        total = acc[half, 0, 0:8, :]
        for row in range(8, span, 8):
            total = total + acc[half, 0, row : row + 8, :]
        out_sums[half] = total
    sum_copies = []
    for index, (step, flip) in enumerate(others):
        slot = step * 2 + flip
        sum_copies.append(
            pltpu.make_async_remote_copy(
                src_ref=out_sums.at[flip],
                dst_ref=sums.at[slot - 1],
                send_sem=sum_send.at[index],
                recv_sem=sum_recv.at[index],
                device_id=other(step, flip),
                device_id_type=MESH,
            )
        )
    for copy in sum_copies:
        copy.start()

    trials = outer * inner * 2 * local
    pair_copy.wait()
    real = acc[0, 1] + peer_acc[1]
    imag = acc[0, 2] + peer_acc[2]
    itc_ref[...] = (real * real + imag * imag) / trials
    power = (acc[0, 0] + peer_acc[0]) / trials
    total = out_sums[0]
    for index, copy in enumerate(sum_copies):
        copy.wait()
        total = total + sums[index]
    mean_power = jnp.sum(total, axis=0, keepdims=True) / trials / (span * groups)
    rel_ref[...] = power / (mean_power + MEAN_EPSILON)

    def drain(e, carry):
        oa = e // inner
        ob = e % inner
        for chunk in range(chunks):
            inner_sends(oa, ob, chunk, finish)

            @pl.when(ob == b)
            def _():
                outer_sends(oa, chunk, finish)

        return carry

    lax.fori_loop(0, outer * inner, drain, 0)


def shards(signals, kernel, freqs):
    local, chans, samples = signals.shape
    sources = kernel.shape[0]
    span = freqs.shape[0] * TOUT
    groups = lax.axis_size("freq")
    chips = lax.axis_size("trial") // 2
    outer, inner = grid_of(chips)
    main = chans // LANES * LANES
    width = local * main + LANES
    depth = 2 * (main + LANES)
    chunks = 2
    vmem = pl.BlockSpec(memory_space=pltpu.VMEM)
    out = jax.ShapeDtypeStruct((span, sources), F32)
    dma = pltpu.SemaphoreType.DMA
    rel_power, itc_score = pl.pallas_call(
        functools.partial(body, outer, inner, groups),
        out_shape=(out, out),
        in_specs=[pl.BlockSpec(memory_space=pltpu.SMEM), vmem, vmem],
        out_specs=(vmem, vmem),
        scratch_shapes=[
            pltpu.VMEM((4 * span, samples), BF16),
            pltpu.VMEM((LANES, samples), BF16),
            pltpu.VMEM((chips, chunks, 2 * span, width), BF16),
            pltpu.VMEM((sources, chans), BF16),
            pltpu.VMEM((sources, LANES), F32),
            pltpu.VMEM((local, depth, 2 * sources), BF16),
            pltpu.VMEM((2, 3, span, sources), F32),
            pltpu.VMEM((3, span, sources), F32),
            pltpu.VMEM((2 * groups - 1, 8, sources), F32),
            pltpu.VMEM((2, 8, sources), F32),
            dma((chips, chunks)),
            dma((2, outer, chunks)),
            dma((2, chips, chunks)),
            dma((2,)),
            dma((2,)),
            dma((2 * groups - 1,)),
            dma((2 * groups - 1,)),
        ],
        compiler_params=pltpu.CompilerParams(collective_id=0, has_side_effects=True),
    )(freqs, signals, kernel)
    return rel_power.T, itc_score.T


def solution(mesh):
    return jax.shard_map(
        shards,
        mesh=mesh,
        in_specs=(P("trial", None, None), P("trial", None), P("freq")),
        out_specs=(P("trial", "freq"), P("trial", "freq")),
        check_vma=False,
    )
```

time: 113 us -> 57 us (0.50)
  waiting for transfers between devices: 73.9 us -> 0 us
  Pallas kernels: 0 us -> 48.3 us
  between operations: 14.1 us -> 0.64 us
  matrix products: 12 us -> 0 us
  other arithmetic: 5.31 us -> 0 us
  blocking collectives: 4.93 us -> 0 us
  local copies, waits for them, and re-layouts: 3.08 us -> 7.78 us
    all_gather x1 -> x0, waiting for transfers between devices: 73.9 us -> none  [shards(): lax.all_gather(coefficients, 'trial', axis=0, tiled=True)]
    pallas_call x0 -> x1, Pallas kernels: none -> 48.3 us  [shards(): pl.pallas_call(functools.partial(body, outer, inner, groups), out_shape=(...]
    dot_general x2 -> x0, matrix products: 12 us -> none  [the longest x1 10.6 us: source_terms(): jnp.einsum('sc,ncm->snm', kernel_rows.astype(jnp.float32), coefficients,...]
    unnamed x3 -> x4, local copies, waits for them, and re-layouts: 1.64 us -> 7.78 us
    psum x1 -> x0, blocking collectives: 4.93 us -> none  [shards(): source_sum = lax.psum(jnp.sum(power, axis=1), 'freq')]
    mul x3 -> x0, other arithmetic: 2.05 us -> none  [the longest x1 1.27 us: wavelet_table(): envelope * jnp.cos(angles)]
    reduce_sum x2 -> x0, other arithmetic: 1.81 us -> none  [the longest x1 1.78 us: source_terms(): jnp.sum(real_part * inverse, axis=1)]
    reshape x3 -> x0, local copies, waits for them, and re-layouts: 1.44 us -> none  [the longest x2 1.19 us: shards(): coefficients = coefficients.reshape(trial_count, chan_count, 2 * span)]
  transfers between devices with their start and end apart: 1 -> 0, of which waited for: 1 -> 0; matrix products, arithmetic and copies ran while one was open for 0% -> 0% of each run, Pallas kernels for 0% -> 0%
where the time goes in v1:
time: 57 us; the launch traced here: 56.7 us
  Pallas kernels  48.3 us (85%)
  local copies, waits for them, and re-layouts  7.78 us (14%)
  between operations  0.64 us (1%)
    pallas_call x1, Pallas kernels, shards(): pl.pallas_call(functools.partial(body, outer, inner, groups), out_shape=(...  48.3 us
    unnamed x4, local copies, waits for them, and re-layouts  7.78 us

profile of v1, /device:TPU:0, one launch (start us, length us, event | category | flops | bytes accessed | tf_op | source)
XLA Modules:
  0.0 56.7 jit_solution(8488752639001298661)
XLA Ops:
  0.6 1.9 %copy.6.kernel_ref = bf16[512,306]{1,0:T(8,128)(2,1)} copy(bf16[512,306]{0,1:T(8,128)(2,1)} %param.4) | data formatting | bytes 626688 | tf_op args[1]
  2.5 2.7 %copy.5.signals_ref = bf16[2,306,1024]{2,1,0:T(8,128)(2,1)} copy(bf16[2,306,1024]{2,0,1:T(2,128)(2,1)} %param.3) | data formatting | bytes 2506752 | tf_op args[0]
  5.2 48.3 %shard_map.50 = (f32[80,512]{1,0:T(8,128)}, f32[80,512]{1,0:T(8,128)}) custom-call(f32[5]{0:T(128)} %freqs_ref.1, bf16[2,306,1024]{2,1,0:T(8,128)(2,1)} %copy.5.signals_ref, bf16[512,306]{1,0:T(8,128)(2,1)} %copy.6.kernel_ref), custom_call_target="tpu_custom_call" | custom-call | tf_op jit(solution)/shard_map/pallas_call | solution.py:409
  53.5 1.6 %copy.9 = f32[512,80]{0,1:T(8,128)} copy(f32[512,80]{0,1:T(8,128)} %bitcast.3) | data formatting | bytes 327680
  55.1 1.6 %copy.10 = f32[512,80]{0,1:T(8,128)} copy(f32[512,80]{0,1:T(8,128)} %bitcast.2) | data formatting | bytes 327680

commit v2 on v1

--- a/solution.py
+++ b/solution.py
@@ -60,12 +60,23 @@
     return high, (x - high.astype(F32)).astype(BF16)
 
 
-def encode(rows):
-    return split(rows)
-
-
-def decode(block):
-    return block[0], block[1]
+POWER_LOG = 4
+CODE_TOP = 2.0 ** (125.0 / 2**POWER_LOG)
+
+
+def encode(rows, inverse):
+    x = rows * inverse
+    y = x * x
+    for _ in range(POWER_LOG - 1):
+        y = y * y
+    return jnp.where(x < 0, -y, y).astype(BF16)
+
+
+def decode(code, scale):
+    y = code.astype(F32)
+    size = jnp.maximum(jnp.abs(y), 1.2e-38)
+    x = jnp.exp(jnp.log(size) * (1.0 / 2**POWER_LOG)) * scale
+    return jnp.where(y < 0, -x, jnp.where(y > 0, x, 0.0))
 
 
 def body(
@@ -77,7 +88,9 @@
     kernel_ref,
     rel_ref,
     itc_ref,
+    mean_ref,
     table,
+    plain,
     rest_rows,
     blocks,
     peer_kernel,
@@ -96,7 +109,7 @@
     sum_recv,
 ):
     local, chans, samples = signals_ref.shape
-    sources = kernel_ref.shape[0]
+    sources = kernel_ref.shape[1]
     bands = freqs_ref.shape[0]
     span = bands * TOUT
     main = chans // LANES * LANES
@@ -177,13 +190,24 @@
     mine = a * inner + b
     pieces = [(j * main, main, functools.partial(lambda j: signals_ref[j, 0:main, :], j)) for j in range(local)]
     pieces.append((local * main, LANES, lambda: rest_rows[...]))
+    top = jnp.zeros((2 * span, 1), F32)
     for start, width, load in pieces:
         both = lax.dot_general(
             table[...], load(), (((1,), (1,)), ((), ())), preferred_element_type=F32
         )
-        coded = encode(both[: 2 * span] + both[2 * span :])
-        for chunk in range(chunks):
-            blocks[mine, chunk, :, start : start + width] = coded[chunk]
+        value = both[: 2 * span] + both[2 * span :]
+        plain[:, start : start + width] = value
+        top = jnp.maximum(top, jnp.max(jnp.abs(value), axis=1, keepdims=True))
+    scale = jnp.maximum(top * 1.01, 1e-30).astype(BF16)
+    inverse = CODE_TOP / scale.astype(F32)
+    lane = lax.broadcasted_iota(jnp.int32, (span, LANES), 1)
+    for chunk in range(chunks):
+        rows = slice(chunk * span, (chunk + 1) * span)
+        for start, width, _ in pieces:
+            coded = encode(plain[rows, start : start + width], inverse[rows])
+            if start == local * main:
+                coded = jnp.where(lane == rest, scale[rows].astype(F32), coded.astype(F32)).astype(BF16)
+            blocks[mine, chunk, :, start : start + width] = coded
 
     def outer_copy(oa, chunk, ahead):
         slot = oa * inner + b
@@ -248,10 +272,10 @@
     acc[...] = jnp.zeros_like(acc)
 
     def place_weights(ref, first):
-        wide = ref[:, 0:main].astype(F32).T.astype(BF16)
+        wide = ref[0:main, :]
         rest_pad[...] = jnp.zeros_like(rest_pad)
-        rest_pad[:, 0:rest] = ref[:, main:chans].astype(F32)
-        tail = rest_pad[...].T.astype(BF16)[0:slot_rows]
+        rest_pad[0:rest, :] = ref[main:chans, :]
+        tail = rest_pad[...]
         cols = slice(first, first + sources)
         for j in range(local):
             for copy in range(2):
@@ -269,7 +293,13 @@
     tiles = sources // step_lanes
 
     def compute(slot):
-        high, low = decode([blocks[slot, chunk] for chunk in range(chunks)])
+        values = []
+        for chunk in range(chunks):
+            code = blocks[slot, chunk]
+            at_scale = local * main + rest
+            scale = code[:, at_scale : at_scale + 1].astype(F32) * (1.0 / CODE_TOP)
+            values.append(decode(code, scale))
+        high, low = split(jnp.concatenate(values, axis=0))
         tail = local * main
         for j in range(local):
             left = jnp.concatenate(
@@ -368,14 +398,13 @@
     pair_copy.wait()
     real = acc[0, 1] + peer_acc[1]
     imag = acc[0, 2] + peer_acc[2]
-    itc_ref[...] = (real * real + imag * imag) / trials
-    power = (acc[0, 0] + peer_acc[0]) / trials
+    itc_ref[...] = real * real + imag * imag
+    rel_ref[...] = (acc[0, 0] + peer_acc[0]) / trials
     total = out_sums[0]
     for index, copy in enumerate(sum_copies):
         copy.wait()
         total = total + sums[index]
-    mean_power = jnp.sum(total, axis=0, keepdims=True) / trials / (span * groups)
-    rel_ref[...] = power / (mean_power + MEAN_EPSILON)
+    mean_ref[...] = jnp.sum(total, axis=0, keepdims=True) / trials / (span * groups)
 
     def drain(e, carry):
         oa = e // inner
@@ -406,17 +435,18 @@
     vmem = pl.BlockSpec(memory_space=pltpu.VMEM)
     out = jax.ShapeDtypeStruct((span, sources), F32)
     dma = pltpu.SemaphoreType.DMA
-    rel_power, itc_score = pl.pallas_call(
+    power, phase, mean_power = pl.pallas_call(
         functools.partial(body, outer, inner, groups),
-        out_shape=(out, out),
+        out_shape=(out, out, jax.ShapeDtypeStruct((1, sources), F32)),
         in_specs=[pl.BlockSpec(memory_space=pltpu.SMEM), vmem, vmem],
-        out_specs=(vmem, vmem),
+        out_specs=(vmem, vmem, vmem),
         scratch_shapes=[
             pltpu.VMEM((4 * span, samples), BF16),
+            pltpu.VMEM((2 * span, width), F32),
             pltpu.VMEM((LANES, samples), BF16),
-            pltpu.VMEM((chips, chunks, 2 * span, width), BF16),
-            pltpu.VMEM((sources, chans), BF16),
-            pltpu.VMEM((sources, LANES), F32),
+            pltpu.VMEM((chips, chunks, span, width), BF16),
+            pltpu.VMEM((chans, sources), BF16),
+            pltpu.VMEM((LANES // local, sources), BF16),
             pltpu.VMEM((local, depth, 2 * sources), BF16),
             pltpu.VMEM((2, 3, span, sources), F32),
             pltpu.VMEM((3, span, sources), F32),
@@ -431,7 +461,9 @@
             dma((2 * groups - 1,)),
         ],
         compiler_params=pltpu.CompilerParams(collective_id=0, has_side_effects=True),
-    )(freqs, signals, kernel)
+    )(freqs, signals, kernel.T)
+    rel_power = power / (mean_power + MEAN_EPSILON)
+    itc_score = phase / (chips * 2 * local)
     return rel_power.T, itc_score.T
 
 

time: 57 us -> 39.9 us (0.70)
  Pallas kernels: 48.3 us -> 34 us
  local copies, waits for them, and re-layouts: 7.78 us -> 2.68 us
  other arithmetic: 0 us -> 2.42 us
    pallas_call x1, Pallas kernels: 48.3 us -> 34 us  [shards(): pl.pallas_call(functools.partial(body, outer, inner, groups), out_shape=(...]
    unnamed x4 -> x1, local copies, waits for them, and re-layouts: 7.78 us -> 2.68 us
    transpose x0 -> x1, other arithmetic: none -> 1.74 us  [shards(): return (rel_power.T, itc_score.T)]
    add x0 -> x1, other arithmetic: none -> 0.68 us  [shards(): rel_power = power / (mean_power + MEAN_EPSILON)]
where the time goes in v2:
time: 39.9 us; the launch traced here: 39.7 us
  Pallas kernels  34 us (85%)
  local copies, waits for them, and re-layouts  2.68 us (7%)
  other arithmetic  2.42 us (6%)
  between operations  0.64 us (2%)
    pallas_call x1, Pallas kernels, shards(): pl.pallas_call(functools.partial(body, outer, inner, groups), out_shape=(...  34 us
    unnamed x1, local copies, waits for them, and re-layouts  2.68 us
    transpose x1, other arithmetic, shards(): return (rel_power.T, itc_score.T)  1.74 us

profile of v2, /device:TPU:0, one launch (start us, length us, event | category | flops | bytes accessed | tf_op | source)
XLA Modules:
  0.0 39.7 jit_solution(10616363434481001990)
XLA Ops:
  0.6 2.7 %copy.5.signals_ref = bf16[2,306,1024]{2,1,0:T(8,128)(2,1)} copy(bf16[2,306,1024]{2,0,1:T(2,128)(2,1)} %param.3) | data formatting | bytes 2506752 | tf_op args[0]
  3.3 34.0 %shard_map.50 = (f32[80,512]{1,0:T(8,128)}, f32[80,512]{1,0:T(8,128)}, f32[1,512]{1,0:T(1,128)}) custom-call(f32[5]{0:T(128)} %freqs_ref.1, bf16[2,306,1024]{2,1,0:T(8,128)(2,1)} %copy.5.signals_ref, bf16[306,512]{1,0:T(8,128)(2,1)} %bitcast.6), custom_call_target="tpu_custom_call" | custom-call | tf_op jit(solution)/shard_map/pallas_call | solution.py:438
  37.3 0.7 %broadcast_add_fusion = f32[1,512]{1,0:T(1,128)S(1)} fusion(f32[1,512]{1,0:T(1,128)} %get-tuple-element.6), kind=kLoop, calls=%fused_computation.2 | loop fusion | flops 512 | bytes 4096 | tf_op jit(solution)/shard_map/add | solution.py:465
  38.0 1.7 %multiply_bitcast_fusion = (f32[512,80]{0,1:T(8,128)}, f32[512,80]{0,1:T(8,128)}) fusion(f32[80,512]{1,0:T(8,128)} %get-tuple-element.7, f32[80,512]{1,0:T(8,128)} %get-tuple-element.5, f32[512]{0:T(512)S(1)} %bitcast.7), kind=kLoop, calls=%fused_computation | loop fusion | flops 81920 | bytes 657408 | tf_op jit(solution)/shard_map/transpose | solution.py:467

commit v3 on v2

--- a/solution.py
+++ b/solution.py
@@ -55,6 +55,14 @@
     )
 
 
+def row_parts(rows):
+    unit = 16
+    crossed = rows // 5 // unit * unit
+    rest = rows - crossed
+    half = -(-rest // 2 // unit) * unit
+    return ((0, crossed, True), (crossed, half, False), (crossed + half, rest - half, False))
+
+
 def split(x):
     high = x.astype(BF16)
     return high, (x - high.astype(F32)).astype(BF16)
@@ -84,11 +92,14 @@
     inner,
     groups,
     freqs_ref,
-    signals_ref,
-    kernel_ref,
+    signals_hbm,
+    kernel_hbm,
     rel_ref,
     itc_ref,
     mean_ref,
+    signals_ref,
+    kernel_ref,
+    load_sem,
     table,
     plain,
     rest_rows,
@@ -108,6 +119,10 @@
     sum_send,
     sum_recv,
 ):
+    signals_load = pltpu.make_async_copy(signals_hbm, signals_ref, load_sem.at[0])
+    signals_load.start()
+    kernel_load = pltpu.make_async_copy(kernel_hbm, kernel_ref, load_sem.at[1])
+    kernel_load.start()
     local, chans, samples = signals_ref.shape
     sources = kernel_ref.shape[1]
     bands = freqs_ref.shape[0]
@@ -115,7 +130,8 @@
     main = chans // LANES * LANES
     rest = chans - main
     slot_rows = LANES // local
-    chunks = blocks.shape[1]
+    parts = row_parts(2 * span)
+    chunks = len(parts)
 
     group = lax.axis_index("freq")
     place = lax.axis_index("trial")
@@ -167,7 +183,7 @@
     pl.semaphore_wait(barrier, near + len(others))
 
     kernel_copy = pltpu.make_async_remote_copy(
-        src_ref=kernel_ref,
+        src_ref=kernel_hbm,
         dst_ref=peer_kernel,
         send_sem=pair_send.at[0],
         recv_sem=pair_recv.at[0],
@@ -184,6 +200,7 @@
             table[first : first + TOUT, :] = high
             table[2 * span + first : 2 * span + first + TOUT, :] = low
     rest_rows[...] = jnp.zeros_like(rest_rows)
+    signals_load.wait()
     for j in range(local):
         rest_rows[j * slot_rows : j * slot_rows + rest, :] = signals_ref[j, main:chans, :]
 
@@ -200,56 +217,39 @@
         top = jnp.maximum(top, jnp.max(jnp.abs(value), axis=1, keepdims=True))
     scale = jnp.maximum(top * 1.01, 1e-30).astype(BF16)
     inverse = CODE_TOP / scale.astype(F32)
-    lane = lax.broadcasted_iota(jnp.int32, (span, LANES), 1)
-    for chunk in range(chunks):
-        rows = slice(chunk * span, (chunk + 1) * span)
-        for start, width, _ in pieces:
-            coded = encode(plain[rows, start : start + width], inverse[rows])
-            if start == local * main:
-                coded = jnp.where(lane == rest, scale[rows].astype(F32), coded.astype(F32)).astype(BF16)
-            blocks[mine, chunk, :, start : start + width] = coded
-
-    def outer_copy(oa, chunk, ahead):
-        slot = oa * inner + b
-        side = (ahead + 1) // 2
+    def neighbour_copy(slot, chunk, sems, ahead, target):
+        first, count, _ = parts[chunk]
+        rows = pl.ds(first, count)
         return pltpu.make_async_remote_copy(
-            src_ref=blocks.at[slot, chunk],
-            dst_ref=blocks.at[slot, chunk],
-            send_sem=outer_send.at[side, oa, chunk],
+            src_ref=blocks.at[slot, rows],
+            dst_ref=blocks.at[slot, rows],
+            send_sem=sems.at[(ahead + 1) // 2, slot, chunk],
             recv_sem=recv.at[slot, chunk],
-            device_id={"trial": at(a + ahead, b)},
+            device_id={"trial": target},
             device_id_type=MESH,
         )
 
-    def inner_copy(oa, ob, chunk, ahead):
+    def sends(oa, ob, chunk, act):
         slot = oa * inner + ob
-        side = (ahead + 1) // 2
-        return pltpu.make_async_remote_copy(
-            src_ref=blocks.at[slot, chunk],
-            dst_ref=blocks.at[slot, chunk],
-            send_sem=inner_send.at[side, slot, chunk],
-            recv_sem=recv.at[slot, chunk],
-            device_id={"trial": at(a, b + ahead)},
-            device_id_type=MESH,
-        )
-
-    def outer_sends(oa, chunk, act):
-        @pl.when((oa <= a) & (a + 1 < outer))
-        def _():
-            act(outer_copy(oa, chunk, 1))
-
-        @pl.when((oa >= a) & (a >= 1))
-        def _():
-            act(outer_copy(oa, chunk, -1))
-
-    def inner_sends(oa, ob, chunk, act):
-        @pl.when((ob <= b) & (b + 1 < inner))
-        def _():
-            act(inner_copy(oa, ob, chunk, 1))
-
-        @pl.when((ob >= b) & (b >= 1))
-        def _():
-            act(inner_copy(oa, ob, chunk, -1))
+        inner_first = parts[chunk][2]
+        along_outer = (oa >= 0) if inner_first else (ob == b)
+        along_inner = (oa == a) if inner_first else (oa >= 0)
+
+        @pl.when(along_outer & (oa <= a) & (a + 1 < outer))
+        def _():
+            act(neighbour_copy(slot, chunk, outer_send, 1, at(a + 1, b)))
+
+        @pl.when(along_outer & (oa >= a) & (a >= 1))
+        def _():
+            act(neighbour_copy(slot, chunk, outer_send, -1, at(a - 1, b)))
+
+        @pl.when(along_inner & (ob <= b) & (b + 1 < inner))
+        def _():
+            act(neighbour_copy(slot, chunk, inner_send, 1, at(a, b + 1)))
+
+        @pl.when(along_inner & (ob >= b) & (b >= 1))
+        def _():
+            act(neighbour_copy(slot, chunk, inner_send, -1, at(a, b - 1)))
 
     def start(copy):
         copy.start()
@@ -265,9 +265,15 @@
         to_left = jnp.where(k <= both, k % 2, jnp.where(left > right, 1, 0))
         return here + dist - 2 * dist * to_left
 
-    for chunk in range(chunks):
-        outer_sends(a, chunk, start)
-        inner_sends(a, b, chunk, start)
+    for chunk, (first, count, _) in enumerate(parts):
+        rows = slice(first, first + count)
+        lane = lax.broadcasted_iota(jnp.int32, (count, LANES), 1)
+        for at_lane, width, _ in pieces:
+            coded = encode(plain[rows, at_lane : at_lane + width], inverse[rows])
+            if at_lane == local * main:
+                coded = jnp.where(lane == rest, scale[rows].astype(F32), coded.astype(F32)).astype(BF16)
+            blocks[mine, rows, at_lane : at_lane + width] = coded
+        sends(a, b, chunk, start)
 
     acc[...] = jnp.zeros_like(acc)
 
@@ -285,6 +291,7 @@
                     rows = slice(base + other_slot * slot_rows, base + (other_slot + 1) * slot_rows)
                     weights[j, rows, cols] = tail if other_slot == j else jnp.zeros_like(tail)
 
+    kernel_load.wait()
     place_weights(kernel_ref, 0)
     kernel_copy.wait()
     place_weights(peer_kernel, sources)
@@ -292,15 +299,21 @@
     step_lanes = min(256, sources)
     tiles = sources // step_lanes
 
-    def compute(slot):
-        values = []
-        for chunk in range(chunks):
-            code = blocks[slot, chunk]
-            at_scale = local * main + rest
-            scale = code[:, at_scale : at_scale + 1].astype(F32) * (1.0 / CODE_TOP)
-            values.append(decode(code, scale))
-        high, low = split(jnp.concatenate(values, axis=0))
+    pair_copy = pltpu.make_async_remote_copy(
+        src_ref=acc.at[1],
+        dst_ref=peer_acc,
+        send_sem=pair_send.at[1],
+        recv_sem=pair_recv.at[1],
+        device_id={"trial": partner},
+        device_id_type=MESH,
+    )
+
+    def compute(slot, last):
+        code = blocks[slot]
         tail = local * main
+        scale = code[:, tail + rest : tail + rest + 1].astype(F32) * (1.0 / CODE_TOP)
+        high, low = split(decode(code, scale))
+        lefts = []
         for j in range(local):
             left = jnp.concatenate(
                 [
@@ -311,12 +324,14 @@
                 ],
                 axis=1,
             )
-            for half in range(2):
+            lefts.append(left)
+        for half in (1, 0):
+            for j in range(local):
                 for tile in range(tiles):
                     lanes = slice(tile * step_lanes, (tile + 1) * step_lanes)
                     first = half * sources + tile * step_lanes
                     source = jnp.dot(
-                        left,
+                        lefts[j],
                         weights[j, :, first : first + step_lanes],
                         preferred_element_type=F32,
                     )
@@ -327,11 +342,18 @@
                     acc[half, 0, :, lanes] += magnitude
                     acc[half, 1, :, lanes] += real * inverse
                     acc[half, 2, :, lanes] += imag * inverse
+            if half:
+
+                @pl.when(last)
+                def _():
+                    pair_copy.start()
 
     def arrived(slot, chunk):
+        first, count, _ = parts[chunk]
+        rows = pl.ds(first, count)
         pltpu.make_async_remote_copy(
-            src_ref=blocks.at[slot, chunk],
-            dst_ref=blocks.at[slot, chunk],
+            src_ref=blocks.at[slot, rows],
+            dst_ref=blocks.at[slot, rows],
             send_sem=pair_send.at[0],
             recv_sem=recv.at[slot, chunk],
             device_id={"trial": partner},
@@ -348,31 +370,21 @@
         def _():
             for chunk in range(chunks):
                 arrived(oa * inner + ob, chunk)
-                inner_sends(oa, ob, chunk, start)
-
-        compute(oa * inner + ob)
+                sends(oa, ob, chunk, start)
+
+        compute(oa * inner + ob, e == outer * inner - 1)
 
         @pl.when((kb == 0) & (ka + 1 < outer))
         def _():
             na = nearest(ka + 1, a, outer)
             for chunk in range(chunks):
                 arrived(na * inner + b, chunk)
-                outer_sends(na, chunk, start)
-                inner_sends(na, b, chunk, start)
+                sends(na, b, chunk, start)
 
         return carry
 
     lax.fori_loop(0, outer * inner, event, 0)
 
-    pair_copy = pltpu.make_async_remote_copy(
-        src_ref=acc.at[1],
-        dst_ref=peer_acc,
-        send_sem=pair_send.at[1],
-        recv_sem=pair_recv.at[1],
-        device_id={"trial": partner},
-        device_id_type=MESH,
-    )
-    pair_copy.start()
     for half in range(2):
         total = acc[half, 0, 0:8, :]
         for row in range(8, span, 8):
@@ -404,17 +416,14 @@
     for index, copy in enumerate(sum_copies):
         copy.wait()
         total = total + sums[index]
-    mean_ref[...] = jnp.sum(total, axis=0, keepdims=True) / trials / (span * groups)
+    mean_power = jnp.sum(total, axis=0, keepdims=True) / trials / (span * groups)
+    mean_ref[...] = mean_power + MEAN_EPSILON
 
     def drain(e, carry):
         oa = e // inner
         ob = e % inner
         for chunk in range(chunks):
-            inner_sends(oa, ob, chunk, finish)
-
-            @pl.when(ob == b)
-            def _():
-                outer_sends(oa, chunk, finish)
+            sends(oa, ob, chunk, finish)
 
         return carry
 
@@ -431,20 +440,24 @@
     main = chans // LANES * LANES
     width = local * main + LANES
     depth = 2 * (main + LANES)
-    chunks = 2
+    chunks = len(row_parts(2 * span))
+    hbm = pl.BlockSpec(memory_space=pl.ANY)
     vmem = pl.BlockSpec(memory_space=pltpu.VMEM)
     out = jax.ShapeDtypeStruct((span, sources), F32)
     dma = pltpu.SemaphoreType.DMA
     power, phase, mean_power = pl.pallas_call(
         functools.partial(body, outer, inner, groups),
         out_shape=(out, out, jax.ShapeDtypeStruct((1, sources), F32)),
-        in_specs=[pl.BlockSpec(memory_space=pltpu.SMEM), vmem, vmem],
+        in_specs=[pl.BlockSpec(memory_space=pltpu.SMEM), hbm, hbm],
         out_specs=(vmem, vmem, vmem),
         scratch_shapes=[
+            pltpu.VMEM((local, chans, samples), BF16),
+            pltpu.VMEM((chans, sources), BF16),
+            dma((2,)),
             pltpu.VMEM((4 * span, samples), BF16),
             pltpu.VMEM((2 * span, width), F32),
             pltpu.VMEM((LANES, samples), BF16),
-            pltpu.VMEM((chips, chunks, span, width), BF16),
+            pltpu.VMEM((chips, 2 * span, width), BF16),
             pltpu.VMEM((chans, sources), BF16),
             pltpu.VMEM((LANES // local, sources), BF16),
             pltpu.VMEM((local, depth, 2 * sources), BF16),
@@ -453,7 +466,7 @@
             pltpu.VMEM((2 * groups - 1, 8, sources), F32),
             pltpu.VMEM((2, 8, sources), F32),
             dma((chips, chunks)),
-            dma((2, outer, chunks)),
+            dma((2, chips, chunks)),
             dma((2, chips, chunks)),
             dma((2,)),
             dma((2,)),
@@ -462,7 +475,7 @@
         ],
         compiler_params=pltpu.CompilerParams(collective_id=0, has_side_effects=True),
     )(freqs, signals, kernel.T)
-    rel_power = power / (mean_power + MEAN_EPSILON)
+    rel_power = power / mean_power
     itc_score = phase / (chips * 2 * local)
     return rel_power.T, itc_score.T
 

time: 39.9 us -> 40.2 us (level)
  Pallas kernels: 34 us -> 35 us
  other arithmetic: 2.42 us -> 1.74 us
    pallas_call x1, Pallas kernels: 34 us -> 35 us  [shards(): pl.pallas_call(functools.partial(body, outer, inner, groups), out_shape=(...]
    add x1 -> x0, other arithmetic: 0.68 us -> none  [shards(): rel_power = power / (mean_power + MEAN_EPSILON)]
where the time goes in v3:
time: 40.2 us; the launch traced here: 40 us
  Pallas kernels  35 us (87%)
  local copies, waits for them, and re-layouts  2.68 us (7%)
  other arithmetic  1.74 us (4%)
  between operations  0.64 us (2%)
    pallas_call x1, Pallas kernels, shards(): pl.pallas_call(functools.partial(body, outer, inner, groups), out_shape=(...  35 us
    unnamed x1, local copies, waits for them, and re-layouts  2.68 us
    transpose x1, other arithmetic, shards(): return (rel_power.T, itc_score.T)  1.74 us

profile of v3, /device:TPU:0, one launch (start us, length us, event | category | flops | bytes accessed | tf_op | source)
XLA Modules:
  0.0 40.0 jit_solution(11773357968525910758)
XLA Ops:
  0.6 2.7 %copy.5.signals_hbm = bf16[2,306,1024]{2,1,0:T(8,128)(2,1)} copy(bf16[2,306,1024]{2,0,1:T(2,128)(2,1)} %param.3) | data formatting | bytes 2506752 | tf_op args[0]
  3.3 35.0 %shard_map.50 = (f32[80,512]{1,0:T(8,128)}, f32[80,512]{1,0:T(8,128)}, f32[1,512]{1,0:T(1,128)}) custom-call(f32[5]{0:T(128)} %freqs_ref.1, bf16[2,306,1024]{2,1,0:T(8,128)(2,1)} %copy.5.signals_hbm, bf16[306,512]{1,0:T(8,128)(2,1)} %bitcast.6), custom_call_target="tpu_custom_call" | custom-call | tf_op jit(solution)/shard_map/pallas_call | solution.py:448
  38.3 1.7 %multiply_bitcast_fusion = (f32[512,80]{0,1:T(8,128)}, f32[512,80]{0,1:T(8,128)}) fusion(f32[80,512]{1,0:T(8,128)} %get-tuple-element.7, f32[80,512]{1,0:T(8,128)} %get-tuple-element.5, f32[512]{0:T(512)} %bitcast.7), kind=kLoop, calls=%fused_computation | loop fusion | flops 81920 | bytes 657408 | tf_op jit(solution)/shard_map/transpose | solution.py:480

commit v4 on v3

--- a/solution.py
+++ b/solution.py
@@ -57,10 +57,8 @@
 
 def row_parts(rows):
     unit = 16
-    crossed = rows // 5 // unit * unit
-    rest = rows - crossed
-    half = -(-rest // 2 // unit) * unit
-    return ((0, crossed, True), (crossed, half, False), (crossed + half, rest - half, False))
+    half = rows // 2 // unit * unit
+    return ((0, half, False), (half, rows - half, False))
 
 
 def split(x):
@@ -360,30 +358,46 @@
             device_id_type=MESH,
         ).wait_recv()
 
+    reach = jnp.maximum(a, outer - 1 - a)
+    last_side = jnp.where((outer - 1 - a == reach) & (reach > 0), 1, 0)
+
+    def origin(dist, side):
+        there = a - dist + 2 * dist * side
+        exists = (there >= 0) & (there < outer) & ((dist > 0) | (side == 0))
+        return there, exists
+
     def event(e, carry):
-        ka = e // inner
-        kb = e % inner
-        oa = nearest(ka, a, outer)
+        dist = e // (2 * inner)
+        kb = e % (2 * inner) // 2
+        side = e % 2
+        oa, exists = origin(dist, side)
         ob = nearest(kb, b, inner)
 
-        @pl.when(kb > 0)
+        @pl.when(exists)
+        def _():
+            @pl.when(kb > 0)
+            def _():
+                for chunk in range(chunks):
+                    arrived(oa * inner + ob, chunk)
+                    sends(oa, ob, chunk, start)
+
+            last = (dist == reach) & (kb == inner - 1) & (side == last_side)
+            compute(oa * inner + ob, last)
+
+        @pl.when((kb == 0) & (side == 1))
         def _():
             for chunk in range(chunks):
-                arrived(oa * inner + ob, chunk)
-                sends(oa, ob, chunk, start)
-
-        compute(oa * inner + ob, e == outer * inner - 1)
-
-        @pl.when((kb == 0) & (ka + 1 < outer))
-        def _():
-            na = nearest(ka + 1, a, outer)
-            for chunk in range(chunks):
-                arrived(na * inner + b, chunk)
-                sends(na, b, chunk, start)
+                for next_side in range(2):
+                    na, more = origin(dist + 1, next_side)
+
+                    @pl.when(more)
+                    def _():
+                        arrived(na * inner + b, chunk)
+                        sends(na, b, chunk, start)
 
         return carry
 
-    lax.fori_loop(0, outer * inner, event, 0)
+    lax.fori_loop(0, outer * inner * 2, event, 0)
 
     for half in range(2):
         total = acc[half, 0, 0:8, :]

time: 40.2 us -> 36.7 us (0.913)
  Pallas kernels: 35 us -> 31.4 us
    pallas_call x1, Pallas kernels: 35 us -> 31.4 us  [shards(): pl.pallas_call(functools.partial(body, outer, inner, groups), out_shape=(...]
where the time goes in v4:
time: 36.7 us; the launch traced here: 36.5 us
  Pallas kernels  31.4 us (86%)
  local copies, waits for them, and re-layouts  2.68 us (7%)
  other arithmetic  1.74 us (5%)
  between operations  0.64 us (2%)
    pallas_call x1, Pallas kernels, shards(): pl.pallas_call(functools.partial(body, outer, inner, groups), out_shape=(...  31.4 us
    unnamed x1, local copies, waits for them, and re-layouts  2.68 us
    transpose x1, other arithmetic, shards(): return (rel_power.T, itc_score.T)  1.74 us

profile of v4, /device:TPU:0, one launch (start us, length us, event | category | flops | bytes accessed | tf_op | source)
XLA Modules:
  0.0 36.5 jit_solution(11984580392001366030)
XLA Ops:
  0.6 2.7 %copy.5.signals_hbm = bf16[2,306,1024]{2,1,0:T(8,128)(2,1)} copy(bf16[2,306,1024]{2,0,1:T(2,128)(2,1)} %param.3) | data formatting | bytes 2506752 | tf_op args[0]
  3.3 31.4 %shard_map.50 = (f32[80,512]{1,0:T(8,128)}, f32[80,512]{1,0:T(8,128)}, f32[1,512]{1,0:T(1,128)}) custom-call(f32[5]{0:T(128)} %freqs_ref.1, bf16[2,306,1024]{2,1,0:T(8,128)(2,1)} %copy.5.signals_hbm, bf16[306,512]{1,0:T(8,128)(2,1)} %bitcast.6), custom_call_target="tpu_custom_call" | custom-call | tf_op jit(solution)/shard_map/pallas_call | solution.py:462
  34.8 1.7 %multiply_bitcast_fusion = (f32[512,80]{0,1:T(8,128)}, f32[512,80]{0,1:T(8,128)}) fusion(f32[80,512]{1,0:T(8,128)} %get-tuple-element.7, f32[80,512]{1,0:T(8,128)} %get-tuple-element.5, f32[512]{0:T(512)} %bitcast.7), kind=kLoop, calls=%fused_computation | loop fusion | flops 81920 | bytes 657408 | tf_op jit(solution)/shard_map/transpose | solution.py:494
